TPU v7x, 256 devices: a whole 4x4x8 slice. The times are simulated.
256 devices in a mesh: section: 8 (over z_hi, core), tp: 32 (over z_lo, x, y).
Axes of the slice: x: 4, y: 4, z: 8 (z_hi: 4, z_lo: 2; z = z_hi * 2 + z_lo), core: 2. Of those that a mesh axis runs over, the one named last changes fastest.
Arguments:
- start_tokens: bfloat16 [2, 32, 8192], P(None, None, 'tp'), may hold values from -6 to 6
- target_weight: bfloat16 [8, 8192, 8192], P('section', None, 'tp'), may hold values from -0.0625 to 0.0625
- online_weight: bfloat16 [8, 8192, 8192], P('section', 'tp'), may hold values from -0.0625 to 0.0625
- head_weight: bfloat16 [8192, 256], P('tp'), may hold values from -0.0625 to 0.0625
- reward: float32 [2, 32], P(None, 'section'), may hold values from -6 to 6
- action_bin: int32 [2, 32], P(None, 'section'), may hold values from 0 to 255
Outputs:
- target_value: float32 [2, 32], P(None, 'section')
- q_taken: float32 [2, 32], P(None, 'section')
All inputs are finite; a program needn't handle non-finite values.
Results may differ from a plain program's by a relative error of at most 0.018.
Values may be sent and summed in bfloat16 or wider, within the bound.
A program may use at most 64 MiB of HBM per device.

v0:
```python
import jax
import jax.numpy as jnp
from jax import lax
from jax.sharding import PartitionSpec as P


def shifted(block, axis, distance):
    devices = range(lax.axis_size(axis))
    route = [(i - distance, i) for i in devices if i - distance in devices]
    return lax.ppermute(block, axis, route)


def from_root(value, axis, source):
    kept = jnp.where(lax.axis_index(axis) == source, value, 0).astype(value.dtype)
    return lax.psum(kept, axis)


def per_device(start_tokens, target_weight, online_weight, head_weight, reward, action_bin):
    moved = lax.all_to_all(online_weight, "tp", split_axis=2, concat_axis=1, tiled=True)
    blended = (0.25 * moved.astype(jnp.float32) + 0.75 * target_weight.astype(jnp.float32)).astype(
        jnp.bfloat16
    )[0]
    sections = lax.axis_size("section")
    position = lax.axis_index("section")
    micro = start_tokens.shape[0]
    finished = jnp.zeros(start_tokens.shape, jnp.bfloat16)
    incoming = jnp.zeros(start_tokens.shape[1:], jnp.bfloat16)

    def advance(tick, carry):
        incoming, finished = carry
        fresh = lax.dynamic_index_in_dim(
            start_tokens, jnp.minimum(tick, micro - 1), 0, keepdims=False
        )
        source = jnp.where(position == 0, fresh, incoming)
        local = source.astype(jnp.float32)
        whole = lax.all_gather(source, "tp", axis=1, tiled=True)
        wide = whole.astype(jnp.float32)
        normed = (wide * lax.rsqrt(jnp.mean(wide * wide, axis=1, keepdims=True) + 1e-06)).astype(
            jnp.bfloat16
        )
        result = (local + jnp.dot(normed, blended, preferred_element_type=jnp.float32)).astype(
            jnp.bfloat16
        )
        slot = tick - (sections - 1)
        keep = jnp.logical_and(position == sections - 1, slot >= 0)
        placed = lax.dynamic_update_index_in_dim(finished, result, jnp.clip(slot, 0, micro - 1), 0)
        finished = jnp.where(keep, placed, finished)
        incoming = shifted(result, "section", 1)
        return (incoming, finished)

    incoming, finished = lax.fori_loop(0, micro + sections - 1, advance, (incoming, finished))
    outputs = from_root(finished, "section", sections - 1)
    share_rows = reward.shape[1]
    mine = lax.dynamic_slice_in_dim(outputs, position * share_rows, share_rows, 1)
    mine = mine.reshape(micro * share_rows, mine.shape[2])
    partial_value = jnp.dot(mine, head_weight, preferred_element_type=jnp.float32)
    actions = action_bin.reshape(micro * share_rows, 1)
    values = lax.psum(partial_value, "tp")
    best = jnp.max(values, axis=1)
    chosen = (jnp.arange(values.shape[1], dtype=jnp.int32)[None, :] == actions).astype(jnp.float32)
    taken = jnp.sum(values * chosen, axis=1)
    best = best.reshape(micro, share_rows)
    taken = taken.reshape(micro, share_rows)
    return (reward + 0.98 * best, taken)


def solution(mesh):
    in_specs = (
        P(None, None, "tp"),
        P("section", None, "tp"),
        P("section", "tp", None),
        P("tp", None),
        P(None, "section"),
        P(None, "section"),
    )
    out_specs = (P(None, "section"), P(None, "section"))
    return jax.shard_map(
        per_device, mesh=mesh, in_specs=in_specs, out_specs=out_specs, check_vma=False
    )
```

profile of v0, /device:TPU:136, one launch (start us, length us, event | category | flops | bytes accessed | tf_op | source)
XLA Modules:
  0.0 1105.1 jit_solution(2322913025078302848)
XLA Ops:
  0.6 17.9 %copy.9 = bf16[1,256,8192]{1,0,2:T(2,128)(2,1)} copy(bf16[1,256,8192]{2,1,0:T(8,128)(2,1)} %param.10) | data formatting | bytes 8388608 | tf_op args[2]
  19.0 43.5 %reduce = bf16[8192,256]{1,0:T(8,128)(2,1)} reduce(bf16[8192,1,256]{2,1,0:T(2,128)(2,1)} %bitcast.27, bf16[]{:T(256)} %broadcast.66), dimensions={1}, to_apply=%bitcast.14.reduce_sub_computation | reduce | bytes 8388610
  62.5 6.9 reshape.50
  69.5 8.0 all-to-all-start
  77.6 50.6 %all-to-all-done = bf16[32,2,32768]{2,1,0:T(2,128)(2,1)} async-done(((bf16[32,2,32768]{2,1,0:T(2,128)(2,1)}), bf16[32,2,32768]{2,1,0:T(2,128)(2,1)}, u32[]{:S(2)}, u32[]{:S(2)}) %all-to-all-start) | async-done | bytes 4194336 | tf_op jit(solution)/shard_map/all_to_all | solution.py:19
  128.2 19.8 %reshape.51 = bf16[8192,1,256]{2,1,0:T(2,128)(2,1)} reshape(bf16[32,2,32768]{2,1,0:T(2,128)(2,1)} %all-to-all-done) | data formatting | bytes 8388608
  148.0 10.9 convert_multiply_fusion.2
  158.8 19.2 %copy.10 = f32[1,32,256,256]{3,2,1,0:T(8,128)} copy(f32[1,32,256,256]{2,0,3,1:T(1,128)} %bitcast.28) | data formatting | bytes 16777216 | tf_op jit(solution)/shard_map/mul | solution.py:20
  178.0 7.5 fusion.6
  185.6 810.7 %while.17 = (s32[]{:T(128)}, bf16[32,256]{1,0:T(8,128)(2,1)S(1)}, bf16[2,32,256]{2,1,0:T(8,128)(2,1)S(1)}, pred[]{:T(512)}, bf16[2,32,256]{2,1,0:T(8,128)(2,1)S(...) while((s32[]{:T(128)}, bf16[32,256]{1,0:T(8,128)(2,1)S(1)}, ...), condition=%wide.region_2.3_spmd, body=%wide.region_0.2_spmd.sunk | while | flops 135831600 | bytes 5964925 | solution.py:51
  185.6 80.7 %all_gather.11 = bf16[32,8192]{1,0:T(8,128)(2,1)S(1)} all-gather(bf16[32,256]{1,0:T(8,128)(2,1)S(1)} %bitcast_select_fusion.3), channel_id=1, replica_groups=mesh['section'=8,'tp'=32] {'tp'}, dimensions={1}, use_global_device_ids=true | all-gather | bytes 540672 | tf_op jit(solution)/shard_map/while/body/eval_jaxpr/all_gather | solution.py:36
  271.5 5.2 collective-permute-done
  276.8 83.2 %all_gather.11 = bf16[32,8192]{1,0:T(8,128)(2,1)S(1)} all-gather(bf16[32,256]{1,0:T(8,128)(2,1)S(1)} %bitcast_select_fusion.3), channel_id=1, replica_groups=mesh['section'=8,'tp'=32] {'tp'}, dimensions={1}, use_global_device_ids=true | all-gather | bytes 540672 | tf_op jit(solution)/shard_map/while/body/eval_jaxpr/all_gather | solution.py:36
  365.2 5.2 collective-permute-done
  370.5 78.1 %all_gather.11 = bf16[32,8192]{1,0:T(8,128)(2,1)S(1)} all-gather(bf16[32,256]{1,0:T(8,128)(2,1)S(1)} %bitcast_select_fusion.3), channel_id=1, replica_groups=mesh['section'=8,'tp'=32] {'tp'}, dimensions={1}, use_global_device_ids=true | all-gather | bytes 540672 | tf_op jit(solution)/shard_map/while/body/eval_jaxpr/all_gather | solution.py:36
  453.8 5.2 collective-permute-done
  459.1 80.0 %all_gather.11 = bf16[32,8192]{1,0:T(8,128)(2,1)S(1)} all-gather(bf16[32,256]{1,0:T(8,128)(2,1)S(1)} %bitcast_select_fusion.3), channel_id=1, replica_groups=mesh['section'=8,'tp'=32] {'tp'}, dimensions={1}, use_global_device_ids=true | all-gather | bytes 540672 | tf_op jit(solution)/shard_map/while/body/eval_jaxpr/all_gather | solution.py:36
  544.3 5.2 collective-permute-done
  549.5 78.2 %all_gather.11 = bf16[32,8192]{1,0:T(8,128)(2,1)S(1)} all-gather(bf16[32,256]{1,0:T(8,128)(2,1)S(1)} %bitcast_select_fusion.3), channel_id=1, replica_groups=mesh['section'=8,'tp'=32] {'tp'}, dimensions={1}, use_global_device_ids=true | all-gather | bytes 540672 | tf_op jit(solution)/shard_map/while/body/eval_jaxpr/all_gather | solution.py:36
  627.9 3.1 fusion.16
  632.9 5.2 collective-permute-done
  638.2 79.9 %all_gather.11 = bf16[32,8192]{1,0:T(8,128)(2,1)S(1)} all-gather(bf16[32,256]{1,0:T(8,128)(2,1)S(1)} %bitcast_select_fusion.3), channel_id=1, replica_groups=mesh['section'=8,'tp'=32] {'tp'}, dimensions={1}, use_global_device_ids=true | all-gather | bytes 540672 | tf_op jit(solution)/shard_map/while/body/eval_jaxpr/all_gather | solution.py:36
  718.4 3.1 fusion.16
  723.4 5.2 collective-permute-done
  728.6 78.1 %all_gather.11 = bf16[32,8192]{1,0:T(8,128)(2,1)S(1)} all-gather(bf16[32,256]{1,0:T(8,128)(2,1)S(1)} %bitcast_select_fusion.3), channel_id=1, replica_groups=mesh['section'=8,'tp'=32] {'tp'}, dimensions={1}, use_global_device_ids=true | all-gather | bytes 540672 | tf_op jit(solution)/shard_map/while/body/eval_jaxpr/all_gather | solution.py:36
  812.0 5.2 collective-permute-done
  817.2 80.0 %all_gather.11 = bf16[32,8192]{1,0:T(8,128)(2,1)S(1)} all-gather(bf16[32,256]{1,0:T(8,128)(2,1)S(1)} %bitcast_select_fusion.3), channel_id=1, replica_groups=mesh['section'=8,'tp'=32] {'tp'}, dimensions={1}, use_global_device_ids=true | all-gather | bytes 540672 | tf_op jit(solution)/shard_map/while/body/eval_jaxpr/all_gather | solution.py:36
  902.5 5.2 collective-permute-done
  907.7 78.0 %all_gather.11 = bf16[32,8192]{1,0:T(8,128)(2,1)S(1)} all-gather(bf16[32,256]{1,0:T(8,128)(2,1)S(1)} %bitcast_select_fusion.3), channel_id=1, replica_groups=mesh['section'=8,'tp'=32] {'tp'}, dimensions={1}, use_global_device_ids=true | all-gather | bytes 540672 | tf_op jit(solution)/shard_map/while/body/eval_jaxpr/all_gather | solution.py:36
  991.0 5.2 collective-permute-done
  996.3 27.2 %psum.14 = bf16[2,32,256]{2,1,0:T(8,128)(2,1)S(1)} all-reduce(bf16[2,32,256]{2,1,0:T(8,128)(2,1)S(1)} %broadcast_select_fusion), channel_id=1, replica_groups=mesh['section'=8,'tp'=32] {'section'}, use_global_device_ids=true, to_apply=%region_3.4 | all-reduce | flops 16384 | bytes 65536 | tf_op jit(solution)/shard_map/psum | solution.py:15
  1023.7 80.0 %psum.15 = f32[8,256]{1,0:T(8,128)S(1)} all-reduce(f32[8,256]{1,0:T(8,128)S(1)} %fusion.7), channel_id=1, replica_groups=mesh['section'=8,'tp'=32] {'tp'}, use_global_device_ids=true, to_apply=%region_4.5 | all-reduce | flops 2048 | bytes 16384 | tf_op jit(solution)/shard_map/psum | solution.py:58
  (64 shorter events, 43.3 us)
Async XLA Ops:
  0.6 1022.9 %copy-start = (bf16[256,256]{1,0:T(8,128)(2,1)S(1)}, bf16[256,256]{1,0:T(8,128)(2,1)}, u32[]{:S(2)}) copy-start(bf16[256,256]{1,0:T(8,128)(2,1)} %param.11) | copy-start | bytes 393220
  62.5 15.0 %copy-start.3 = (s32[2,4]{1,0:T(2,128)S(1)}, s32[2,4]{1,0:T(2,128)}, u32[]{:S(2)}) copy-start(s32[2,4]{1,0:T(2,128)} %param.13) | copy-start | bytes 100
  69.5 58.7 %all-to-all-start = ((bf16[32,2,32768]{2,1,0:T(2,128)(2,1)}), bf16[32,2,32768]{2,1,0:T(2,128)(2,1)}, u32[]{:S(2)}, u32[]{:S(2)}) async-start(bf16[32,2,32768]{2,1,0:T(2,128)(2,1)} %reshape.50), calls=%async_computation | async-start | bytes 8388608 | tf_op jit(solution)/shard_map/all_to_all | solution.py:19
  178.0 7.5 copy-start.1
  185.6 919.0 %copy-start.2 = (f32[2,4]{1,0:T(2,128)S(1)}, f32[2,4]{1,0:T(2,128)}, u32[]{:S(2)}) copy-start(f32[2,4]{1,0:T(2,128)} %param.12) | copy-start | bytes 100
  269.6 7.2 collective-permute-start
  363.3 7.2 collective-permute-start
  451.9 7.2 collective-permute-start
  542.3 7.2 collective-permute-start
  631.0 7.2 collective-permute-start
  721.5 7.2 collective-permute-start
  810.0 7.2 collective-permute-start
  900.6 7.2 collective-permute-start
  989.1 7.2 collective-permute-start
where the time goes:
time: 1110 us
  blocking collectives  823 us (74%)
  waiting for transfers between devices  97.7 us (9%)
  local copies, waits for them, and re-layouts  65.1 us (6%)
  other arithmetic  64.9 us (6%)
  matrix products  27.7 us (2%)
  starting transfers between devices  25.3 us (2%)
    all_gather x9, blocking collectives, advance(): whole = lax.all_gather(source, 'tp', axis=1, tiled=True)  716 us
    psum x1, blocking collectives, per_device(): values = lax.psum(partial_value, 'tp')  80 us
    all_to_all x1, waiting for transfers between devices, per_device(): lax.all_to_all(online_weight, 'tp', split_axis=2, concat_axis=1, tiled=True)  50.6 us
    ppermute x9, waiting for transfers between devices, shifted(): return lax.ppermute(block, axis, route)  47.1 us
    unnamed x12, local copies, waits for them, and re-layouts  45.1 us
    unnamed x1, other arithmetic  43.5 us
    dot_general x9, matrix products, advance(): jnp.dot(normed, blended, preferred_element_type=jnp.float32)  27.6 us
    psum x1, blocking collectives, from_root(): return lax.psum(kept, axis)  27.2 us
  transfers between devices with their start and end apart: 10, of which 10 were waited for; matrix products, arithmetic and copies ran while one was open for 0% of the time, Pallas kernels for 0%

commit v1 on v0

--- a/solution.py
+++ b/solution.py
@@ -33,7 +33,9 @@
         )
         source = jnp.where(position == 0, fresh, incoming)
         local = source.astype(jnp.float32)
-        whole = lax.all_gather(source, "tp", axis=1, tiled=True)
+        whole = jnp.concatenate(
+            lax.all_to_all(jnp.stack([source] * lax.axis_size("tp")), "tp", 0, 0), axis=1
+        )
         wide = whole.astype(jnp.float32)
         normed = (wide * lax.rsqrt(jnp.mean(wide * wide, axis=1, keepdims=True) + 1e-06)).astype(
             jnp.bfloat16

time: 1110 us -> 540 us (0.49)
  blocking collectives: 823 us -> 106 us
  waiting for transfers between devices: 97.7 us -> 179 us
  starting transfers between devices: 25.3 us -> 79.9 us
    all_gather x9 -> x0, blocking collectives: 716 us -> none  [advance(): whole = lax.all_gather(source, 'tp', axis=1, tiled=True)]
    all_to_all x0 -> x9, waiting for transfers between devices: none -> 81.6 us  [advance(): lax.all_to_all(jnp.stack([source] * lax.axis_size('tp')), 'tp', 0, 0)]
    all_to_all x0 -> x9, starting transfers between devices: none -> 54.6 us  [advance(): lax.all_to_all(jnp.stack([source] * lax.axis_size('tp')), 'tp', 0, 0)]
  transfers between devices with their start and end apart: 10 -> 19, of which waited for: 10 -> 19; matrix products, arithmetic and copies ran while one was open for 0% -> 0% of each run, Pallas kernels for 0% -> 0%
where the time goes in v1:
time: 540 us; the launch traced here: 534 us
  waiting for transfers between devices  179 us (33%)
  blocking collectives  106 us (20%)
  starting transfers between devices  79.9 us (15%)
  local copies, waits for them, and re-layouts  73.5 us (14%)
  other arithmetic  65.9 us (12%)
  matrix products  27.8 us (5%)
    all_to_all x9, waiting for transfers between devices, advance(): lax.all_to_all(jnp.stack([source] * lax.axis_size('tp')), 'tp', 0, 0)  81.6 us
    psum x1, blocking collectives, per_device(): values = lax.psum(partial_value, 'tp')  79.3 us
    all_to_all x9, starting transfers between devices, advance(): lax.all_to_all(jnp.stack([source] * lax.axis_size('tp')), 'tp', 0, 0)  54.6 us
    all_to_all x1, waiting for transfers between devices, per_device(): lax.all_to_all(online_weight, 'tp', split_axis=2, concat_axis=1, tiled=True)  50.6 us
    ppermute x9, waiting for transfers between devices, shifted(): return lax.ppermute(block, axis, route)  47.1 us
    unnamed x12, local copies, waits for them, and re-layouts  45.1 us
    unnamed x1, other arithmetic  43.5 us
    dot_general x9, matrix products, advance(): jnp.dot(normed, blended, preferred_element_type=jnp.float32)  27.7 us
  transfers between devices with their start and end apart: 19, of which 19 were waited for; matrix products, arithmetic and copies ran while one was open for 0% of the time, Pallas kernels for 0%

profile of v1, /device:TPU:136, one launch (start us, length us, event | category | flops | bytes accessed | tf_op | source)
XLA Modules:
  0.0 534.2 jit_solution(8261143864675311437)
XLA Ops:
  0.6 17.9 %copy.11 = bf16[1,256,8192]{1,0,2:T(2,128)(2,1)} copy(bf16[1,256,8192]{2,1,0:T(8,128)(2,1)} %param.10) | data formatting | bytes 8388608 | tf_op args[2]
  19.0 43.5 %reduce.2 = bf16[8192,256]{1,0:T(8,128)(2,1)} reduce(bf16[8192,1,256]{2,1,0:T(2,128)(2,1)} %bitcast.36, bf16[]{:T(256)} %broadcast.73), dimensions={1}, to_apply=%bitcast.18.reduce_sub_computation | reduce | bytes 8388610
  62.5 6.9 %reshape.71 = bf16[32,2,32768]{2,1,0:T(2,128)(2,1)} reshape(bf16[8192,256]{1,0:T(8,128)(2,1)} %reduce.2) | data formatting | bytes 8388608
  69.5 8.0 %all-to-all-start.1 = ((bf16[32,2,32768]{2,1,0:T(2,128)(2,1)}), bf16[32,2,32768]{2,1,0:T(2,128)(2,1)}, u32[]{:S(2)}, u32[]{:S(2)}) async-start(bf16[32,2,32768]{2,1,0:T(2,128)(2,1)} %reshape.71), calls=%async_computation.1 | async-start | bytes 8388608 | tf_op jit(solution)/shard_map/all_to_all | solution.py:19
  77.6 50.6 %all-to-all-done.1 = bf16[32,2,32768]{2,1,0:T(2,128)(2,1)} async-done(((bf16[32,2,32768]{2,1,0:T(2,128)(2,1)}), bf16[32,2,32768]{2,1,0:T(2,128)(2,1)}, u32[]{:S(2)}, u32[]{:S(2)}) %all-to-all-start.1) | async-done | bytes 4194336 | tf_op jit(solution)/shard_map/all_to_all | solution.py:19
  128.2 19.8 %reshape.72 = bf16[8192,1,256]{2,1,0:T(2,128)(2,1)} reshape(bf16[32,2,32768]{2,1,0:T(2,128)(2,1)} %all-to-all-done.1) | data formatting | bytes 8388608
  148.0 10.9 %convert_multiply_fusion.1 = f32[1,256,8192]{1,0,2:T(1,128)} fusion(bf16[8192,1,256]{2,1,0:T(2,128)(2,1)} %reshape.72), kind=kLoop, calls=%fused_computation.13 | loop fusion | flops 4194304 | bytes 12582912 | tf_op jit(solution)/shard_map/mul | solution.py:20
  158.8 19.2 %copy.12 = f32[1,32,256,256]{3,2,1,0:T(8,128)} copy(f32[1,32,256,256]{2,0,3,1:T(1,128)} %bitcast.37) | data formatting | bytes 16777216 | tf_op jit(solution)/shard_map/mul | solution.py:20
  178.0 7.5 %fusion.4 = bf16[1,8192,256]{2,1,0:T(8,128)(2,1)} fusion(f32[1,32,256,256]{3,2,1,0:T(8,128)} %copy.12, bf16[1,8192,256]{2,1,0:T(8,128)(2,1)} %param.9), kind=kLoop, calls=%fused_computation.12 | loop fusion | flops 8388608 | bytes 16777216 | tf_op jit(solution)/shard_map/convert_element_type | solution.py:20
  185.6 240.5 %while.17 = (s32[]{:T(128)}, bf16[32,256]{1,0:T(8,128)(2,1)S(1)}, bf16[2,32,256]{2,1,0:T(8,128)(2,1)S(1)}, pred[]{:T(512)}, bf16[2,32,256]{2,1,0:T(8,128)(2,1)S(...) while((s32[]{:T(128)}, bf16[32,256]{1,0:T(8,128)(2,1)S(1)}, ...), condition=%wide.region_2.3_spmd, body=%wide.region_0.2_spmd.sunk | while | flops 135831600 | bytes 11732125 | solution.py:53
  186.5 11.4 %all-to-all-start = ((bf16[32,32,256]{2,1,0:T(8,128)(2,1)}), bf16[32,32,256]{2,1,0:T(8,128)(2,1)S(1)}, u32[]{:S(2)}, u32[]{:S(2)}) async-start(bf16[32,32,256]{2,1,0:T(8,128)(2,1)} %stack.7), calls=%async_computation | async-start | bytes 1048576 | tf_op jit(solution)/shard_map/while/body/eval_jaxpr/all_to_all | solution.py:37
  197.9 10.5 %all-to-all-done = bf16[32,32,256]{2,1,0:T(8,128)(2,1)S(1)} async-done(((bf16[32,32,256]{2,1,0:T(8,128)(2,1)}), bf16[32,32,256]{2,1,0:T(8,128)(2,1)S(1)}, u32[]{:S(2)}, u32[]{:S(2)}) %all-to-all-start) | async-done | bytes 524320 | tf_op jit(solution)/shard_map/while/body/eval_jaxpr/all_to_all | solution.py:37
  219.9 5.4 %all-to-all-start = ((bf16[32,32,256]{2,1,0:T(8,128)(2,1)}), bf16[32,32,256]{2,1,0:T(8,128)(2,1)S(1)}, u32[]{:S(2)}, u32[]{:S(2)}) async-start(bf16[32,32,256]{2,1,0:T(8,128)(2,1)} %stack.7), calls=%async_computation | async-start | bytes 1048576 | tf_op jit(solution)/shard_map/while/body/eval_jaxpr/all_to_all | solution.py:37
  225.3 8.9 %all-to-all-done = bf16[32,32,256]{2,1,0:T(8,128)(2,1)S(1)} async-done(((bf16[32,32,256]{2,1,0:T(8,128)(2,1)}), bf16[32,32,256]{2,1,0:T(8,128)(2,1)S(1)}, u32[]{:S(2)}, u32[]{:S(2)}) %all-to-all-start) | async-done | bytes 524320 | tf_op jit(solution)/shard_map/while/body/eval_jaxpr/all_to_all | solution.py:37
  239.7 5.2 collective-permute-done
  245.8 5.4 %all-to-all-start = ((bf16[32,32,256]{2,1,0:T(8,128)(2,1)}), bf16[32,32,256]{2,1,0:T(8,128)(2,1)S(1)}, u32[]{:S(2)}, u32[]{:S(2)}) async-start(bf16[32,32,256]{2,1,0:T(8,128)(2,1)} %stack.7), calls=%async_computation | async-start | bytes 1048576 | tf_op jit(solution)/shard_map/while/body/eval_jaxpr/all_to_all | solution.py:37
  251.2 8.9 %all-to-all-done = bf16[32,32,256]{2,1,0:T(8,128)(2,1)S(1)} async-done(((bf16[32,32,256]{2,1,0:T(8,128)(2,1)}), bf16[32,32,256]{2,1,0:T(8,128)(2,1)S(1)}, u32[]{:S(2)}, u32[]{:S(2)}) %all-to-all-start) | async-done | bytes 524320 | tf_op jit(solution)/shard_map/while/body/eval_jaxpr/all_to_all | solution.py:37
  271.7 5.4 %all-to-all-start = ((bf16[32,32,256]{2,1,0:T(8,128)(2,1)}), bf16[32,32,256]{2,1,0:T(8,128)(2,1)S(1)}, u32[]{:S(2)}, u32[]{:S(2)}) async-start(bf16[32,32,256]{2,1,0:T(8,128)(2,1)} %stack.7), calls=%async_computation | async-start | bytes 1048576 | tf_op jit(solution)/shard_map/while/body/eval_jaxpr/all_to_all | solution.py:37
  277.1 8.9 %all-to-all-done = bf16[32,32,256]{2,1,0:T(8,128)(2,1)S(1)} async-done(((bf16[32,32,256]{2,1,0:T(8,128)(2,1)}), bf16[32,32,256]{2,1,0:T(8,128)(2,1)S(1)}, u32[]{:S(2)}, u32[]{:S(2)}) %all-to-all-start) | async-done | bytes 524320 | tf_op jit(solution)/shard_map/while/body/eval_jaxpr/all_to_all | solution.py:37
  291.5 5.2 collective-permute-done
  297.6 5.4 %all-to-all-start = ((bf16[32,32,256]{2,1,0:T(8,128)(2,1)}), bf16[32,32,256]{2,1,0:T(8,128)(2,1)S(1)}, u32[]{:S(2)}, u32[]{:S(2)}) async-start(bf16[32,32,256]{2,1,0:T(8,128)(2,1)} %stack.7), calls=%async_computation | async-start | bytes 1048576 | tf_op jit(solution)/shard_map/while/body/eval_jaxpr/all_to_all | solution.py:37
  303.0 8.9 %all-to-all-done = bf16[32,32,256]{2,1,0:T(8,128)(2,1)S(1)} async-done(((bf16[32,32,256]{2,1,0:T(8,128)(2,1)}), bf16[32,32,256]{2,1,0:T(8,128)(2,1)S(1)}, u32[]{:S(2)}, u32[]{:S(2)}) %all-to-all-start) | async-done | bytes 524320 | tf_op jit(solution)/shard_map/while/body/eval_jaxpr/all_to_all | solution.py:37
  323.4 5.4 %all-to-all-start = ((bf16[32,32,256]{2,1,0:T(8,128)(2,1)}), bf16[32,32,256]{2,1,0:T(8,128)(2,1)S(1)}, u32[]{:S(2)}, u32[]{:S(2)}) async-start(bf16[32,32,256]{2,1,0:T(8,128)(2,1)} %stack.7), calls=%async_computation | async-start | bytes 1048576 | tf_op jit(solution)/shard_map/while/body/eval_jaxpr/all_to_all | solution.py:37
  328.9 8.9 %all-to-all-done = bf16[32,32,256]{2,1,0:T(8,128)(2,1)S(1)} async-done(((bf16[32,32,256]{2,1,0:T(8,128)(2,1)}), bf16[32,32,256]{2,1,0:T(8,128)(2,1)S(1)}, u32[]{:S(2)}, u32[]{:S(2)}) %all-to-all-start) | async-done | bytes 524320 | tf_op jit(solution)/shard_map/while/body/eval_jaxpr/all_to_all | solution.py:37
  349.3 5.4 %all-to-all-start = ((bf16[32,32,256]{2,1,0:T(8,128)(2,1)}), bf16[32,32,256]{2,1,0:T(8,128)(2,1)S(1)}, u32[]{:S(2)}, u32[]{:S(2)}) async-start(bf16[32,32,256]{2,1,0:T(8,128)(2,1)} %stack.7), calls=%async_computation | async-start | bytes 1048576 | tf_op jit(solution)/shard_map/while/body/eval_jaxpr/all_to_all | solution.py:37
  354.7 8.9 %all-to-all-done = bf16[32,32,256]{2,1,0:T(8,128)(2,1)S(1)} async-done(((bf16[32,32,256]{2,1,0:T(8,128)(2,1)}), bf16[32,32,256]{2,1,0:T(8,128)(2,1)S(1)}, u32[]{:S(2)}, u32[]{:S(2)}) %all-to-all-start) | async-done | bytes 524320 | tf_op jit(solution)/shard_map/while/body/eval_jaxpr/all_to_all | solution.py:37
  375.2 5.4 %all-to-all-start = ((bf16[32,32,256]{2,1,0:T(8,128)(2,1)}), bf16[32,32,256]{2,1,0:T(8,128)(2,1)S(1)}, u32[]{:S(2)}, u32[]{:S(2)}) async-start(bf16[32,32,256]{2,1,0:T(8,128)(2,1)} %stack.7), calls=%async_computation | async-start | bytes 1048576 | tf_op jit(solution)/shard_map/while/body/eval_jaxpr/all_to_all | solution.py:37
  380.6 8.9 %all-to-all-done = bf16[32,32,256]{2,1,0:T(8,128)(2,1)S(1)} async-done(((bf16[32,32,256]{2,1,0:T(8,128)(2,1)}), bf16[32,32,256]{2,1,0:T(8,128)(2,1)S(1)}, u32[]{:S(2)}, u32[]{:S(2)}) %all-to-all-start) | async-done | bytes 524320 | tf_op jit(solution)/shard_map/while/body/eval_jaxpr/all_to_all | solution.py:37
  401.1 5.4 %all-to-all-start = ((bf16[32,32,256]{2,1,0:T(8,128)(2,1)}), bf16[32,32,256]{2,1,0:T(8,128)(2,1)S(1)}, u32[]{:S(2)}, u32[]{:S(2)}) async-start(bf16[32,32,256]{2,1,0:T(8,128)(2,1)} %stack.7), calls=%async_computation | async-start | bytes 1048576 | tf_op jit(solution)/shard_map/while/body/eval_jaxpr/all_to_all | solution.py:37
  406.5 8.9 %all-to-all-done = bf16[32,32,256]{2,1,0:T(8,128)(2,1)S(1)} async-done(((bf16[32,32,256]{2,1,0:T(8,128)(2,1)}), bf16[32,32,256]{2,1,0:T(8,128)(2,1)S(1)}, u32[]{:S(2)}, u32[]{:S(2)}) %all-to-all-start) | async-done | bytes 524320 | tf_op jit(solution)/shard_map/while/body/eval_jaxpr/all_to_all | solution.py:37
  426.1 27.2 %psum.14 = bf16[2,32,256]{2,1,0:T(8,128)(2,1)S(1)} all-reduce(bf16[2,32,256]{2,1,0:T(8,128)(2,1)S(1)} %broadcast_select_fusion), channel_id=1, replica_groups=mesh['section'=8,'tp'=32] {'section'}, use_global_device_ids=true, to_apply=%region_3.4 | all-reduce | flops 16384 | bytes 65536 | tf_op jit(solution)/shard_map/psum | solution.py:15
  453.5 79.3 %psum.15 = f32[8,256]{1,0:T(8,128)S(1)} all-reduce(f32[8,256]{1,0:T(8,128)S(1)} %fusion.5), channel_id=1, replica_groups=mesh['section'=8,'tp'=32] {'tp'}, use_global_device_ids=true, to_apply=%region_4.5 | all-reduce | flops 2048 | bytes 16384 | tf_op jit(solution)/shard_map/psum | solution.py:60
  (100 shorter events, 95.6 us)
Async XLA Ops:
  0.6 452.7 %copy-start = (bf16[256,256]{1,0:T(8,128)(2,1)S(1)}, bf16[256,256]{1,0:T(8,128)(2,1)}, u32[]{:S(2)}) copy-start(bf16[256,256]{1,0:T(8,128)(2,1)} %param.11) | copy-start | bytes 393220
  62.5 15.0 %copy-start.3 = (s32[2,4]{1,0:T(2,128)S(1)}, s32[2,4]{1,0:T(2,128)}, u32[]{:S(2)}) copy-start(s32[2,4]{1,0:T(2,128)} %param.13) | copy-start | bytes 100
  69.5 58.7 %all-to-all-start.1 = ((bf16[32,2,32768]{2,1,0:T(2,128)(2,1)}), bf16[32,2,32768]{2,1,0:T(2,128)(2,1)}, u32[]{:S(2)}, u32[]{:S(2)}) async-start(bf16[32,2,32768]{2,1,0:T(2,128)(2,1)} %reshape.71), calls=%async_computation.1 | async-start | bytes 8388608 | tf_op jit(solution)/shard_map/all_to_all | solution.py:19
  178.0 7.5 %copy-start.1 = (bf16[2,32,256]{2,1,0:T(8,128)(2,1)S(1)}, bf16[2,32,256]{2,1,0:T(8,128)(2,1)}, u32[]{:S(2)}) copy-start(bf16[2,32,256]{2,1,0:T(8,128)(2,1)} %param.8) | copy-start | bytes 98308
  185.6 348.1 %copy-start.2 = (f32[2,4]{1,0:T(2,128)S(1)}, f32[2,4]{1,0:T(2,128)}, u32[]{:S(2)}) copy-start(f32[2,4]{1,0:T(2,128)} %param.12) | copy-start | bytes 100
  186.5 21.9 %all-to-all-start = ((bf16[32,32,256]{2,1,0:T(8,128)(2,1)}), bf16[32,32,256]{2,1,0:T(8,128)(2,1)S(1)}, u32[]{:S(2)}, u32[]{:S(2)}) async-start(bf16[32,32,256]{2,1,0:T(8,128)(2,1)} %stack.7), calls=%async_computation | async-start | bytes 1048576 | tf_op jit(solution)/shard_map/while/body/eval_jaxpr/all_to_all | solution.py:37
  211.9 7.2 %collective-permute-start = (bf16[32,256]{1,0:T(8,128)(2,1)S(1)}, bf16[32,256]{1,0:T(8,128)(2,1)S(1)}, u32[]{:S(2)}, u32[]{:S(2)}) collective-permute-start(bf16[32,256]{1,0:T(8,128)(2,1)S(1)} %get-tuple-element.227), channel_id=1, source_target_pairs={{0,32},{32,64},{64,96},{96,128},{128,160},{160,192},{192,224},{1,3... | collective-permute-start | bytes 49160 | tf_op jit(solution)/shard_map/while/body/eval_jaxpr/ppermute | solution.py:10
  219.9 14.3 %all-to-all-start = ((bf16[32,32,256]{2,1,0:T(8,128)(2,1)}), bf16[32,32,256]{2,1,0:T(8,128)(2,1)S(1)}, u32[]{:S(2)}, u32[]{:S(2)}) async-start(bf16[32,32,256]{2,1,0:T(8,128)(2,1)} %stack.7), calls=%async_computation | async-start | bytes 1048576 | tf_op jit(solution)/shard_map/while/body/eval_jaxpr/all_to_all | solution.py:37
  237.8 7.2 %collective-permute-start = (bf16[32,256]{1,0:T(8,128)(2,1)S(1)}, bf16[32,256]{1,0:T(8,128)(2,1)S(1)}, u32[]{:S(2)}, u32[]{:S(2)}) collective-permute-start(bf16[32,256]{1,0:T(8,128)(2,1)S(1)} %get-tuple-element.227), channel_id=1, source_target_pairs={{0,32},{32,64},{64,96},{96,128},{128,160},{160,192},{192,224},{1,3... | collective-permute-start | bytes 49160 | tf_op jit(solution)/shard_map/while/body/eval_jaxpr/ppermute | solution.py:10
  245.8 14.3 %all-to-all-start = ((bf16[32,32,256]{2,1,0:T(8,128)(2,1)}), bf16[32,32,256]{2,1,0:T(8,128)(2,1)S(1)}, u32[]{:S(2)}, u32[]{:S(2)}) async-start(bf16[32,32,256]{2,1,0:T(8,128)(2,1)} %stack.7), calls=%async_computation | async-start | bytes 1048576 | tf_op jit(solution)/shard_map/while/body/eval_jaxpr/all_to_all | solution.py:37
  263.6 7.2 %collective-permute-start = (bf16[32,256]{1,0:T(8,128)(2,1)S(1)}, bf16[32,256]{1,0:T(8,128)(2,1)S(1)}, u32[]{:S(2)}, u32[]{:S(2)}) collective-permute-start(bf16[32,256]{1,0:T(8,128)(2,1)S(1)} %get-tuple-element.227), channel_id=1, source_target_pairs={{0,32},{32,64},{64,96},{96,128},{128,160},{160,192},{192,224},{1,3... | collective-permute-start | bytes 49160 | tf_op jit(solution)/shard_map/while/body/eval_jaxpr/ppermute | solution.py:10
  271.7 14.3 %all-to-all-start = ((bf16[32,32,256]{2,1,0:T(8,128)(2,1)}), bf16[32,32,256]{2,1,0:T(8,128)(2,1)S(1)}, u32[]{:S(2)}, u32[]{:S(2)}) async-start(bf16[32,32,256]{2,1,0:T(8,128)(2,1)} %stack.7), calls=%async_computation | async-start | bytes 1048576 | tf_op jit(solution)/shard_map/while/body/eval_jaxpr/all_to_all | solution.py:37
  289.5 7.2 %collective-permute-start = (bf16[32,256]{1,0:T(8,128)(2,1)S(1)}, bf16[32,256]{1,0:T(8,128)(2,1)S(1)}, u32[]{:S(2)}, u32[]{:S(2)}) collective-permute-start(bf16[32,256]{1,0:T(8,128)(2,1)S(1)} %get-tuple-element.227), channel_id=1, source_target_pairs={{0,32},{32,64},{64,96},{96,128},{128,160},{160,192},{192,224},{1,3... | collective-permute-start | bytes 49160 | tf_op jit(solution)/shard_map/while/body/eval_jaxpr/ppermute | solution.py:10
  297.6 14.3 %all-to-all-start = ((bf16[32,32,256]{2,1,0:T(8,128)(2,1)}), bf16[32,32,256]{2,1,0:T(8,128)(2,1)S(1)}, u32[]{:S(2)}, u32[]{:S(2)}) async-start(bf16[32,32,256]{2,1,0:T(8,128)(2,1)} %stack.7), calls=%async_computation | async-start | bytes 1048576 | tf_op jit(solution)/shard_map/while/body/eval_jaxpr/all_to_all | solution.py:37
  315.4 7.2 %collective-permute-start = (bf16[32,256]{1,0:T(8,128)(2,1)S(1)}, bf16[32,256]{1,0:T(8,128)(2,1)S(1)}, u32[]{:S(2)}, u32[]{:S(2)}) collective-permute-start(bf16[32,256]{1,0:T(8,128)(2,1)S(1)} %get-tuple-element.227), channel_id=1, source_target_pairs={{0,32},{32,64},{64,96},{96,128},{128,160},{160,192},{192,224},{1,3... | collective-permute-start | bytes 49160 | tf_op jit(solution)/shard_map/while/body/eval_jaxpr/ppermute | solution.py:10
  323.4 14.3 %all-to-all-start = ((bf16[32,32,256]{2,1,0:T(8,128)(2,1)}), bf16[32,32,256]{2,1,0:T(8,128)(2,1)S(1)}, u32[]{:S(2)}, u32[]{:S(2)}) async-start(bf16[32,32,256]{2,1,0:T(8,128)(2,1)} %stack.7), calls=%async_computation | async-start | bytes 1048576 | tf_op jit(solution)/shard_map/while/body/eval_jaxpr/all_to_all | solution.py:37
  341.3 7.2 %collective-permute-start = (bf16[32,256]{1,0:T(8,128)(2,1)S(1)}, bf16[32,256]{1,0:T(8,128)(2,1)S(1)}, u32[]{:S(2)}, u32[]{:S(2)}) collective-permute-start(bf16[32,256]{1,0:T(8,128)(2,1)S(1)} %get-tuple-element.227), channel_id=1, source_target_pairs={{0,32},{32,64},{64,96},{96,128},{128,160},{160,192},{192,224},{1,3... | collective-permute-start | bytes 49160 | tf_op jit(solution)/shard_map/while/body/eval_jaxpr/ppermute | solution.py:10
  349.3 14.3 %all-to-all-start = ((bf16[32,32,256]{2,1,0:T(8,128)(2,1)}), bf16[32,32,256]{2,1,0:T(8,128)(2,1)S(1)}, u32[]{:S(2)}, u32[]{:S(2)}) async-start(bf16[32,32,256]{2,1,0:T(8,128)(2,1)} %stack.7), calls=%async_computation | async-start | bytes 1048576 | tf_op jit(solution)/shard_map/while/body/eval_jaxpr/all_to_all | solution.py:37
  367.2 7.2 %collective-permute-start = (bf16[32,256]{1,0:T(8,128)(2,1)S(1)}, bf16[32,256]{1,0:T(8,128)(2,1)S(1)}, u32[]{:S(2)}, u32[]{:S(2)}) collective-permute-start(bf16[32,256]{1,0:T(8,128)(2,1)S(1)} %get-tuple-element.227), channel_id=1, source_target_pairs={{0,32},{32,64},{64,96},{96,128},{128,160},{160,192},{192,224},{1,3... | collective-permute-start | bytes 49160 | tf_op jit(solution)/shard_map/while/body/eval_jaxpr/ppermute | solution.py:10
  375.2 14.3 %all-to-all-start = ((bf16[32,32,256]{2,1,0:T(8,128)(2,1)}), bf16[32,32,256]{2,1,0:T(8,128)(2,1)S(1)}, u32[]{:S(2)}, u32[]{:S(2)}) async-start(bf16[32,32,256]{2,1,0:T(8,128)(2,1)} %stack.7), calls=%async_computation | async-start | bytes 1048576 | tf_op jit(solution)/shard_map/while/body/eval_jaxpr/all_to_all | solution.py:37
  393.0 7.2 %collective-permute-start = (bf16[32,256]{1,0:T(8,128)(2,1)S(1)}, bf16[32,256]{1,0:T(8,128)(2,1)S(1)}, u32[]{:S(2)}, u32[]{:S(2)}) collective-permute-start(bf16[32,256]{1,0:T(8,128)(2,1)S(1)} %get-tuple-element.227), channel_id=1, source_target_pairs={{0,32},{32,64},{64,96},{96,128},{128,160},{160,192},{192,224},{1,3... | collective-permute-start | bytes 49160 | tf_op jit(solution)/shard_map/while/body/eval_jaxpr/ppermute | solution.py:10
  401.1 14.3 %all-to-all-start = ((bf16[32,32,256]{2,1,0:T(8,128)(2,1)}), bf16[32,32,256]{2,1,0:T(8,128)(2,1)S(1)}, u32[]{:S(2)}, u32[]{:S(2)}) async-start(bf16[32,32,256]{2,1,0:T(8,128)(2,1)} %stack.7), calls=%async_computation | async-start | bytes 1048576 | tf_op jit(solution)/shard_map/while/body/eval_jaxpr/all_to_all | solution.py:37
  418.9 7.2 %collective-permute-start = (bf16[32,256]{1,0:T(8,128)(2,1)S(1)}, bf16[32,256]{1,0:T(8,128)(2,1)S(1)}, u32[]{:S(2)}, u32[]{:S(2)}) collective-permute-start(bf16[32,256]{1,0:T(8,128)(2,1)S(1)} %get-tuple-element.227), channel_id=1, source_target_pairs={{0,32},{32,64},{64,96},{96,128},{128,160},{160,192},{192,224},{1,3... | collective-permute-start | bytes 49160 | tf_op jit(solution)/shard_map/while/body/eval_jaxpr/ppermute | solution.py:10
